TPU v7x, 256 devices: a whole 4x4x8 slice. The times are simulated.
256 devices in a mesh: rep: 32 (over x, y, core), tp: 8 (over z).
Axes of the slice: x: 4, y: 4, z: 8, core: 2. Of those that a mesh axis runs over, the one named last changes fastest.
Arguments:
- hidden_in: bfloat16 [3072, 8192], P('rep', 'tp'), may hold values from -6 to 6
- queries: bfloat16 [3072, 8192], P('rep', 'tp'), may hold values from -20 to 20
- cache_keys: bfloat16 [3072, 128, 1024], P('rep', None, 'tp'), may hold values from -6 to 6
- cached_value_rows: bfloat16 [3072, 128, 1024], P('rep', None, 'tp'), may hold values from -6 to 6
- cache_lengths: int32 [3072], P('rep'), may hold values from 1 to 128, 98304 in all
- base_key_matrix: bfloat16 [8192, 1024], P(None, 'tp'), may hold values from -0.0625 to 0.0625
- base_value_matrix: bfloat16 [8192, 1024], P(None, 'tp'), may hold values from -0.0625 to 0.0625
- shrink_weights: bfloat16 [128, 8192, 128], P('rep', 'tp'), may hold values from -0.0625 to 0.0625
- pooled_up_weights: bfloat16 [128, 2, 64, 1024], P('rep', None, None, 'tp'), may hold values from -0.75 to 0.75
- block_owner: int32 [768, 1], P('rep'), may hold values from 0 to 31; in each aligned block of 24 rows (0 to 23, 24 to 47, ...) at most 2 rows name the same one
- block_slot: int32 [768], P('rep'), may hold values from 0 to 3
Outputs:
- new_keys: bfloat16 [3072, 1024], P('rep', 'tp')
- new_values: bfloat16 [3072, 1024], P('rep', 'tp')
- context: bfloat16 [3072, 8192], P('rep', 'tp')
Inputs may be any that keep to these rules, and one draw needn't show every extreme that they name: `block_owner`: among the 24 blocks of one replica group at most 2 name the same owner, and some group in every draw has 2 blocks with one owner.
All inputs are finite; a program needn't handle non-finite values. No bound on the sum of `cache_lengths` on one device may be relied on, other than what follows from the above.
Results may differ from a plain program's by a relative error of at most 0.0055.
Values may be sent and summed in bfloat16 or wider, within the bound.
A program may use at most 128 MiB of HBM per device.

v0:
```python
import jax
import jax.numpy as jnp
from jax import lax
from jax.sharding import PartitionSpec as P

HEAD_SIZE = 128
BLK = 4
adapter_scale = 0.5
masked_score = -1e30


def attend(group_queries, key_cache, value_cache, lengths, fresh_keys, fresh_values):
    rows_here = group_queries.shape[0]
    head_groups = key_cache.shape[2] // HEAD_SIZE
    group_size = group_queries.shape[1] // (head_groups * HEAD_SIZE)
    window = key_cache.shape[1]
    inverse_root = HEAD_SIZE ** (-0.5)
    query_heads = group_queries.reshape(rows_here, head_groups, group_size, HEAD_SIZE)
    key_heads = key_cache.reshape(rows_here, window, head_groups, HEAD_SIZE)
    value_heads = value_cache.reshape(rows_here, window, head_groups, HEAD_SIZE)
    scores = (
        jnp.einsum("rkgd,rtkd->rkgt", query_heads, key_heads, preferred_element_type=jnp.float32)
        * inverse_root
    )
    own_score = (
        jnp.einsum(
            "rkgd,rkd->rkg",
            query_heads,
            fresh_keys.reshape(rows_here, head_groups, HEAD_SIZE),
            preferred_element_type=jnp.float32,
        )
        * inverse_root
    )
    visible = (jnp.arange(window, dtype=jnp.int32)[None, :] < lengths[:, None])[:, None, None, :]
    highest = jnp.maximum(jnp.max(jnp.where(visible, scores, masked_score), axis=-1), own_score)
    exp_terms = jnp.where(visible, jnp.exp(scores - highest[..., None]), 0.0)
    own_term = jnp.exp(own_score - highest)
    denominator = jnp.sum(exp_terms, axis=-1) + own_term
    weights = (exp_terms / denominator[..., None]).astype(jnp.bfloat16)
    own_weight = (own_term / denominator).astype(jnp.bfloat16)
    context = jnp.einsum(
        "rkgt,rtkd->rkgd", weights, value_heads, preferred_element_type=jnp.float32
    )
    context = context + own_weight.astype(jnp.float32)[..., None] * fresh_values.reshape(
        rows_here, head_groups, 1, HEAD_SIZE
    ).astype(jnp.float32)
    return context.reshape(rows_here, -1).astype(jnp.bfloat16)


def earlier_ranks(owners):
    span_count = owners.shape[-1]
    matching = owners[..., :, None] == owners[..., None, :]
    before = jnp.arange(span_count)[:, None] > jnp.arange(span_count)[None, :]
    return jnp.sum((matching & before).astype(jnp.int32), axis=-1)


def slot_layout(owners_all, slots_all, myself, replicas, blocks_here, capacity):
    owners_grid = owners_all.reshape(replicas, blocks_here)
    slots_grid = slots_all.reshape(replicas, blocks_here)
    ranks_grid = earlier_ranks(owners_grid)
    placed = (owners_grid == myself)[:, :, None] & (
        ranks_grid[:, :, None] == jnp.arange(capacity, dtype=jnp.int32)[None, None, :]
    )
    placed_int = placed.astype(jnp.int32)
    slot_index = jnp.sum(placed_int * slots_grid[:, :, None], axis=1).reshape(replicas * capacity)
    return (placed, slot_index)


def adapter_pass(slot_rows, slot_index, shrink_weights, pooled_up_weights, site_sum):
    chosen_shrink = jnp.take(shrink_weights, slot_index, axis=0)
    selected_expand = jnp.take(pooled_up_weights, slot_index, axis=0)
    partial_value = jnp.einsum(
        "snd,sdr->snr", slot_rows, chosen_shrink, preferred_element_type=jnp.float32
    )
    shrunk = site_sum(partial_value).astype(jnp.bfloat16)
    split_halves = shrunk.reshape(shrunk.shape[0], shrunk.shape[1], 2, shrunk.shape[2] // 2)
    summed_terms = jnp.einsum(
        "snkr,skrw->snkw", split_halves, selected_expand, preferred_element_type=jnp.float32
    )
    return (adapter_scale * summed_terms).astype(jnp.bfloat16)


def shards(
    hidden_in,
    queries,
    cache_keys,
    cached_value_rows,
    cache_lengths,
    base_key_matrix,
    base_value_matrix,
    shrink_weights,
    pooled_up_weights,
    block_owner,
    block_slot,
):
    rows_here = hidden_in.shape[0]
    shard_width = hidden_in.shape[1]
    replicas = lax.axis_size("rep")
    myself = lax.axis_index("rep")
    blocks_here = rows_here // BLK
    capacity = max(2, (2 * blocks_here + replicas - 1) // replicas)
    key_row_width = base_key_matrix.shape[1]
    gathered = lax.all_gather(hidden_in, "tp", axis=1, tiled=True)
    base_keys = jnp.dot(gathered, base_key_matrix, preferred_element_type=jnp.float32)
    base_values = jnp.dot(gathered, base_value_matrix, preferred_element_type=jnp.float32)
    owners_all, slots_all = (
        lax.all_gather(block_owner[:, 0], "rep", axis=0, tiled=True),
        lax.all_gather(block_slot, "rep", axis=0, tiled=True),
    )
    placed, slot_index = slot_layout(owners_all, slots_all, myself, replicas, blocks_here, capacity)
    every_row = lax.all_gather(hidden_in, "rep", axis=0, tiled=True)
    same_group = jnp.eye(replicas, dtype=jnp.bfloat16)
    compactor = jnp.einsum("pq,qbc->pcqb", same_group, placed.astype(jnp.bfloat16)).reshape(
        replicas * capacity, replicas * blocks_here
    )
    slot_rows = jnp.dot(
        compactor,
        every_row.reshape(replicas * blocks_here, BLK * shard_width),
        preferred_element_type=jnp.float32,
    ).astype(jnp.bfloat16)
    slot_rows = slot_rows.reshape(replicas * capacity, BLK, shard_width)

    def sum_every(partial_value):
        return lax.psum(partial_value, "tp")

    deltas = adapter_pass(slot_rows, slot_index, shrink_weights, pooled_up_weights, sum_every)
    spread = jnp.einsum(
        "sq,sx->qx",
        compactor,
        deltas.reshape(replicas * capacity, BLK * 2 * key_row_width),
        preferred_element_type=jnp.float32,
    )
    spread = spread.reshape(replicas * rows_here, 2, key_row_width)
    per_row_delta = lax.psum_scatter(
        spread.astype(jnp.bfloat16), "rep", scatter_dimension=0, tiled=True
    ).astype(jnp.float32)
    fresh_keys = (base_keys + per_row_delta[:, 0]).astype(jnp.bfloat16)
    fresh_values = (base_values + per_row_delta[:, 1]).astype(jnp.bfloat16)
    context = attend(
        queries, cache_keys, cached_value_rows, cache_lengths, fresh_keys, fresh_values
    )
    return (fresh_keys, fresh_values, context)


def solution(mesh):
    return jax.shard_map(
        shards,
        mesh=mesh,
        in_specs=(
            P("rep", "tp"),
            P("rep", "tp"),
            P("rep", None, "tp"),
            P("rep", None, "tp"),
            P("rep"),
            P(None, "tp"),
            P(None, "tp"),
            P("rep", "tp", None),
            P("rep", None, None, "tp"),
            P("rep", None),
            P("rep"),
        ),
        out_specs=(P("rep", "tp"), P("rep", "tp"), P("rep", "tp")),
        check_vma=False,
    )
```

profile of v0, /device:TPU:2, one launch (start us, length us, event | category | flops | bytes accessed | tf_op | source)
XLA Modules:
  0.0 236.1 jit_solution(2521708871560459143)
XLA Ops:
  8.8 1.4 dynamic-slice
  10.9 0.9 dynamic-update-slice.1
  12.5 15.9 %all-reduce.2 = (s32[768]{0:T(1024)S(1)}, s32[768]{0:T(1024)S(1)}) all-reduce(s32[768]{0:T(1024)S(1)} %bitcast_dynamic-update-slice_fusion, s32[768]{0:T(1024)S(1)} %dynamic-update-slice.1), channel_id=2, replica_groups=mesh['rep'=32,'tp'=8] {'rep'}, use_global_device_ids=true, to_apply=%add | all-reduce | flops 1536 | bytes 12288
  29.3 1.0 multiply_bitcast_fusion
  30.3 1.7 reshape.170
  32.1 2.1 gather_fusion
  34.2 8.6 %gather_fusion.1 = bf16[64,1024,128]{2,1,0:T(8,128)(2,1)} fusion(bf16[4,1024,128]{2,1,0:T(8,128)(2,1)} %param.18, s32[1024]{0:T(1024)S(1)} %pad_clamp_fusion), kind=kCustom, calls=%fused_computation.1 | custom fusion | bytes 33554688 | tf_op jit(solution)/shard_map/jit(_take)/gather | solution.py:70
  42.8 24.6 %all-gather.6.cloned.1.call-done = bf16[3072,1024]{1,0:T(8,128)(2,1)} async-done(((bf16[96,1024]{1,0:T(8,128)(2,1)}), bf16[3072,1024]{1,0:T(8,128)(2,1)}) %all-gather.6.cloned.1.call-update) | async-done | bytes 6291472 | tf_op jit(solution)/shard_map/all_gather | solution.py:111
  67.4 10.7 %reshape.173 = bf16[768,4096]{1,0:T(8,128)(2,1)} reshape(bf16[3072,1024]{1,0:T(8,128)(2,1)} %all-gather.6.cloned.1.call-done) | data formatting | bytes 12582912 | tf_op jit(solution)/shard_map/reshape | solution.py:118
  78.1 4.8 %convolution_convert_fusion = bf16[64,4096]{1,0:T(8,128)(2,1)} fusion(bf16[64,768]{1,0:T(8,128)(2,1)S(1)} %reshape.170, bf16[768,4096]{1,0:T(8,128)(2,1)} %reshape.173), kind=kOutput, calls=%fused_computation.6 | convolution fusion | flops 402915328 | bytes 6914048 | tf_op jit(solution)/shard_map/dot_general | solution.py:116
  82.9 2.2 reshape.174
  85.1 8.7 %fusion = f32[64,4,128]{2,1,0:T(4,128)S(1)} fusion(bf16[64,4,1024]{2,1,0:T(4,128)(2,1)} %reshape.174, bf16[64,1024,128]{2,1,0:T(8,128)(2,1)} %gather_fusion.1, pred[64]{0:T(512)(128)(4,1)S(1)} %compare_and_fusion), kind=kOutput, calls=%fused_computation.2 | convolution fusion | flops 75497472 | bytes 17432640 | tf_op jit(solution)/shard_map/snd,sdr->snr/dot_general | solution.py:72
  93.7 31.5 %all-reduce.4 = bf16[64,4,128]{2,1,0:T(4,128)(2,1)S(1)} all-reduce(f32[64,4,128]{2,1,0:T(4,128)S(1)} %fusion), channel_id=1, replica_groups=mesh['rep'=32,'tp'=8] {'tp'}, use_global_device_ids=true, to_apply=%region_2.3 | all-reduce | flops 32768 | bytes 196608 | tf_op jit(solution)/shard_map/psum | solution.py:124
  125.3 2.3 fusion.14
  127.8 1.7 convolution_convert_fusion.1
  129.6 3.8 %convert_element_type.61 = bf16[3072,2,128]{2,1,0:T(2,128)(2,1)} reshape(bf16[768,1024]{1,0:T(8,128)(2,1)} %convolution_convert_fusion.1) | data formatting | bytes 3145728 | tf_op jit(solution)/shard_map/convert_element_type | solution.py:135
  133.4 2.8 %copy.30 = bf16[3072,2,128]{2,0,1:T(8,128)(2,1)} copy(bf16[3072,2,128]{2,1,0:T(2,128)(2,1)} %convert_element_type.61) | data formatting | bytes 3145728 | tf_op jit(solution)/shard_map/convert_element_type | solution.py:135
  137.5 2.4 %select_reduce_fusion = (f32[96,8]{1,0:T(8,128)}, f32[96,8,128]{2,1,0:T(8,128)S(1)}) fusion(pred[96,128]{1,0:T(8,128)(4,1)S(1)} %iota_compare_fusion, bf16[96,8,128]{2,1,0:T(8,128)(2,1)S(1)} %bitcast.43, bf16[96,128,128]{2,1,0:T(8,128)(2,1)S(1)} %copy-done), kind=kOutput, calls=%fused_computation.25 | convolution fusion | flops 25459968 | bytes 3750912 | tf_op jit(solution)/shard_map/rkgd,rtkd->rkgt/dot_general | solution.py:22
  140.0 79.3 %reduce-scatter.2.cloned.1.call-done = bf16[96,2,128]{2,0,1:T(8,128)(2,1)} async-done(((bf16[3072,2,128]{2,0,1:T(8,128)(2,1)}), bf16[96,2,128]{2,0,1:T(8,128)(2,1)}) %reduce-scatter.2.cloned.1.call-update) | async-done | bytes 49168 | tf_op jit(solution)/shard_map/reduce_scatter | solution.py:134
  219.3 1.4 convert_element_type.62
  220.8 2.8 %fusion.17 = bf16[96,128]{1,0:T(8,128)(2,1)S(1)} fusion(bf16[96,8192]{1,0:T(8,128)(2,1)} %all-gather.4.cloned.1.call-done, bf16[8192,128]{1,0:T(8,128)(2,1)} %param.16, f32[96,2,128]{2,0,1:T(8,128)} %convert_element_type.62), kind=kOutput, calls=%fused_computation.19 | convolution fusion | flops 201351168 | bytes 3743744 | tf_op jit(solution)/shard_map/dot_general | solution.py:104
  223.6 1.2 fusion.26
  225.1 1.2 fusion.38
  227.0 1.0 fusion.7
  (57 shorter events, 5.7 us)
Async XLA Ops:
  8.0 129.6 %copy-start = (bf16[96,128,128]{2,1,0:T(8,128)(2,1)S(1)}, bf16[96,128,128]{2,1,0:T(8,128)(2,1)}, u32[]{:S(2)}) copy-start(bf16[96,128,128]{2,1,0:T(8,128)(2,1)} %param.13) | copy-start | bytes 9437188
  8.0 24.0 %copy-start.1 = (bf16[4,2,64,128]{3,2,1,0:T(8,128)(2,1)S(1)}, bf16[4,2,64,128]{3,2,1,0:T(8,128)(2,1)}, u32[]{:S(2)}) copy-start(bf16[4,2,64,128]{3,2,1,0:T(8,128)(2,1)} %param.19) | copy-start | bytes 393220
  8.0 59.3 %all-gather.6.cloned.1.call-start = ((), (), s32[]{:S(2)}) async-start(), calls=%async_computation.2 | async-start | bytes 6488064 | tf_op jit(solution)/shard_map/all_gather | solution.py:111
  8.8 210.6 %reduce-scatter.2.cloned.1.call-start = ((), (), s32[]{:S(2)}) async-start(), calls=%async_computation.3 | async-start | bytes 1622016 | tf_op jit(solution)/shard_map/reduce_scatter | solution.py:134
  133.4 3.4 %copy-start.7 = (bf16[96,1024]{1,0:T(8,128)(2,1)S(1)}, bf16[96,1024]{1,0:T(8,128)(2,1)}, u32[]{:S(2)}) copy-start(bf16[96,1024]{1,0:T(8,128)(2,1)} %param.12) | copy-start | bytes 589828
  133.4 3.5 %copy-start.9 = (s32[96]{0:T(128)S(1)}, s32[96]{0:T(128)}, u32[]{:S(2)}) copy-start(s32[96]{0:T(128)} %param.15) | copy-start | bytes 1156
  136.2 84.5 %all-gather.4.cloned.1.call-start = ((), (), s32[]{:S(2)}) async-start(), calls=%async_computation.1 | async-start | bytes 1769472 | tf_op jit(solution)/shard_map/all_gather | solution.py:103
  136.9 0.7 copy-start.4
  220.8 4.0 %copy-start.5 = (f32[96,8]{1,0:T(8,128)S(1)}, f32[96,8]{1,0:T(8,128)}, u32[]{:S(2)}) copy-start(f32[96,8]{1,0:T(8,128)} %get-tuple-element.9) | copy-start | bytes 9220
  220.8 4.4 %copy-start.2 = (bf16[96,8192]{1,0:T(8,128)(2,1)S(1)}, bf16[96,8192]{1,0:T(8,128)(2,1)}, u32[]{:S(2)}) copy-start(bf16[96,8192]{1,0:T(8,128)(2,1)} %all-gather.4.cloned.1.call-done) | copy-start | bytes 4718596
  220.8 4.4 %copy-start.3 = (bf16[8192,128]{1,0:T(8,128)(2,1)S(1)}, bf16[8192,128]{1,0:T(8,128)(2,1)}, u32[]{:S(2)}) copy-start(bf16[8192,128]{1,0:T(8,128)(2,1)} %param.17) | copy-start | bytes 6291460
  220.8 4.4 %copy-start.6 = (f32[96,2,128]{2,0,1:T(8,128)S(1)}, f32[96,2,128]{2,0,1:T(8,128)}, u32[]{:S(2)}) copy-start(f32[96,2,128]{2,0,1:T(8,128)} %convert_element_type.62) | copy-start | bytes 294916
  223.5 2.8 %copy-start.8 = (bf16[96,128]{1,0:T(8,128)(2,1)}, bf16[96,128]{1,0:T(8,128)(2,1)S(1)}, u32[]{:S(2)}) copy-start(bf16[96,128]{1,0:T(8,128)(2,1)S(1)} %fusion.17) | copy-start | bytes 73732
  225.1 1.9 copy-start.10
Sparse Core Ops, SparseCore 0:
  11.4 55.9 all-gather.5
  136.3 82.9 reduce-scatter.1
Sparse Core Ops, SparseCore 1:
  138.5 36.9 all-gather.3
where the time goes:
time: 237 us; the launch traced here: 236 us
  waiting for transfers between devices  105 us (44%)
  blocking collectives  47.3 us (20%)
  local copies, waits for them, and re-layouts  37.9 us (16%)
  matrix products  26 us (11%)
  between operations  16.4 us (7%)
  other arithmetic  3.18 us (1%)
    reduce_scatter x1, waiting for transfers between devices, shards(): lax.psum_scatter(spread.astype(jnp.bfloat16), 'rep', scatter_dimension=0,...  79.3 us
    psum x1, blocking collectives, sum_every(): return lax.psum(partial_value, 'tp')  31.5 us
    all_gather x1, waiting for transfers between devices, shards(): every_row = lax.all_gather(hidden_in, 'rep', axis=0, tiled=True)  24.6 us
    unnamed x1, blocking collectives  15.9 us
    reshape x1, local copies, waits for them, and re-layouts, shards(): every_row.reshape(replicas * blocks_here, BLK * shard_width)  10.7 us
    dot_general x1, matrix products, adapter_pass(): jnp.einsum('snd,sdr->snr', slot_rows, chosen_shrink, preferred_element_ty...  8.66 us
    gather x1, local copies, waits for them, and re-layouts, adapter_pass(): chosen_shrink = jnp.take(shrink_weights, slot_index, axis=0)  8.6 us
    convert_element_type x2, local copies, waits for them, and re-layouts, shards(): spread.astype(jnp.bfloat16)  6.61 us
  transfers between devices with their start and end apart: 3, of which 2 were waited for; matrix products, arithmetic and copies ran while one was open for 9% of the time, Pallas kernels for 0%

commit v1 on v0

--- a/solution.py
+++ b/solution.py
@@ -2,6 +2,7 @@
 import jax.numpy as jnp
 from jax import lax
 from jax.sharding import PartitionSpec as P
+from jax.lax import all_gather
 
 HEAD_SIZE = 128
 BLK = 4
@@ -121,7 +122,11 @@
     slot_rows = slot_rows.reshape(replicas * capacity, BLK, shard_width)
 
     def sum_every(partial_value):
-        return lax.psum(partial_value, "tp")
+
+        def rest_the_slot(v0):
+            return jnp.sum(all_gather(v0, "tp"), 0)
+
+        return rest_the_slot(partial_value)
 
     deltas = adapter_pass(slot_rows, slot_index, shrink_weights, pooled_up_weights, sum_every)
     spread = jnp.einsum(

time: 237 us -> 285 us (1.20)
  waiting for transfers between devices: 105 us -> 184 us
  blocking collectives: 47.3 us -> 15.9 us
    all_gather x1, waiting for transfers between devices: 0.01 us -> 39.5 us  [shards(): gathered = lax.all_gather(hidden_in, 'tp', axis=1, tiled=True)]
    all_gather x0 -> x1, waiting for transfers between devices: none -> 36.2 us  [rest_the_slot(): return jnp.sum(all_gather(v0, 'tp'), 0)]
    psum x1 -> x0, blocking collectives: 31.5 us -> none  [sum_every(): return lax.psum(partial_value, 'tp')]
  transfers between devices with their start and end apart: 3 -> 4, of which waited for: 2 -> 4; matrix products, arithmetic and copies ran while one was open for 9% -> 8% of each run, Pallas kernels for 0% -> 0%
where the time goes in v1:
time: 285 us; the launch traced here: 284 us
  waiting for transfers between devices  184 us (65%)
  local copies, waits for them, and re-layouts  38 us (13%)
  matrix products  26.8 us (9%)
  blocking collectives  15.9 us (6%)
  between operations  14.7 us (5%)
  other arithmetic  4.61 us (2%)
    reduce_scatter x1, waiting for transfers between devices, shards(): lax.psum_scatter(spread.astype(jnp.bfloat16), 'rep', scatter_dimension=0,...  80.5 us
    all_gather x1, waiting for transfers between devices, shards(): gathered = lax.all_gather(hidden_in, 'tp', axis=1, tiled=True)  39.5 us
    all_gather x1, waiting for transfers between devices, rest_the_slot(): return jnp.sum(all_gather(v0, 'tp'), 0)  36.2 us
    all_gather x1, waiting for transfers between devices, shards(): every_row = lax.all_gather(hidden_in, 'rep', axis=0, tiled=True)  26.7 us
    unnamed x1, blocking collectives  15.9 us
    reshape x1, local copies, waits for them, and re-layouts, shards(): every_row.reshape(replicas * blocks_here, BLK * shard_width)  10.7 us
    dot_general x1, matrix products, adapter_pass(): jnp.einsum('snd,sdr->snr', slot_rows, chosen_shrink, preferred_element_ty...  9.36 us
    gather x1, local copies, waits for them, and re-layouts, adapter_pass(): chosen_shrink = jnp.take(shrink_weights, slot_index, axis=0)  8.64 us
  transfers between devices with their start and end apart: 4, of which 4 were waited for; matrix products, arithmetic and copies ran while one was open for 8% of the time, Pallas kernels for 0%

profile of v1, /device:TPU:2, one launch (start us, length us, event | category | flops | bytes accessed | tf_op | source)
XLA Modules:
  0.0 284.2 jit_solution(15611733196950218567)
XLA Ops:
  8.0 1.4 dynamic-slice
  11.6 15.9 %all-reduce.2 = (s32[768]{0:T(1024)S(1)}, s32[768]{0:T(1024)S(1)}) all-reduce(s32[768]{0:T(1024)S(1)} %bitcast_dynamic-update-slice_fusion, s32[768]{0:T(1024)S(1)} %dynamic-update-slice.1), channel_id=2, replica_groups=mesh['rep'=32,'tp'=8] {'rep'}, use_global_device_ids=true, to_apply=%add | all-reduce | flops 1536 | bytes 12288
  29.5 1.7 reshape.170
  31.2 8.6 %gather_fusion.1 = bf16[64,1024,128]{2,1,0:T(8,128)(2,1)} fusion(bf16[4,1024,128]{2,1,0:T(8,128)(2,1)} %param.18, s32[1024]{0:T(1024)S(1)} %pad_clamp_fusion), kind=kCustom, calls=%fused_computation.1 | custom fusion | bytes 33554688 | tf_op jit(solution)/shard_map/jit(_take)/gather | solution.py:71
  39.8 26.7 %all-gather.8.cloned.1.call-done = bf16[3072,1024]{1,0:T(8,128)(2,1)} async-done(((bf16[96,1024]{1,0:T(8,128)(2,1)}), bf16[3072,1024]{1,0:T(8,128)(2,1)}) %all-gather.8.cloned.1.call-update) | async-done | bytes 6291472 | tf_op jit(solution)/shard_map/all_gather | solution.py:112
  66.5 10.7 %reshape.173 = bf16[768,4096]{1,0:T(8,128)(2,1)} reshape(bf16[3072,1024]{1,0:T(8,128)(2,1)} %all-gather.8.cloned.1.call-done) | data formatting | bytes 12582912 | tf_op jit(solution)/shard_map/reshape | solution.py:119
  77.3 4.8 %convolution_convert_fusion = bf16[64,4096]{1,0:T(8,128)(2,1)} fusion(bf16[64,768]{1,0:T(8,128)(2,1)S(1)} %reshape.170, bf16[768,4096]{1,0:T(8,128)(2,1)} %reshape.173), kind=kOutput, calls=%fused_computation.6 | convolution fusion | flops 402915328 | bytes 6914048 | tf_op jit(solution)/shard_map/dot_general | solution.py:117
  82.0 2.2 reshape.174
  84.3 9.4 %fusion = f32[64,4,128]{2,1,0:T(4,128)} fusion(bf16[64,4,1024]{2,1,0:T(4,128)(2,1)} %reshape.174, bf16[64,1024,128]{2,1,0:T(8,128)(2,1)} %gather_fusion.1, pred[64]{0:T(512)(128)(4,1)S(1)} %compare_and_fusion), kind=kOutput, calls=%fused_computation.2 | convolution fusion | flops 75497472 | bytes 17432640 | tf_op jit(solution)/shard_map/snd,sdr->snr/dot_general | solution.py:73
  93.7 2.2 gather_fusion
  95.9 36.2 %all-gather.10.cloned.1.call-done = f32[512,4,128]{2,1,0:T(4,128)} async-done(((f32[64,4,128]{2,1,0:T(4,128)}), f32[512,4,128]{2,1,0:T(4,128)}) %all-gather.10.cloned.1.call-update) | async-done | bytes 1048592 | tf_op jit(solution)/shard_map/all_gather | solution.py:127
  132.1 1.4 reduce_sum.38
  133.6 2.3 fusion.14
  136.1 1.8 convolution_convert_fusion.1
  137.9 3.8 %convert_element_type.66 = bf16[3072,2,128]{2,1,0:T(2,128)(2,1)} reshape(bf16[768,1024]{1,0:T(8,128)(2,1)} %convolution_convert_fusion.1) | data formatting | bytes 3145728 | tf_op jit(solution)/shard_map/convert_element_type | solution.py:140
  141.7 2.8 copy.31
  145.8 2.4 select_reduce_fusion
  148.2 80.5 %reduce-scatter.2.cloned.1.call-done = bf16[96,2,128]{2,0,1:T(8,128)(2,1)} async-done(((bf16[3072,2,128]{2,0,1:T(8,128)(2,1)}), bf16[96,2,128]{2,0,1:T(8,128)(2,1)}) %reduce-scatter.2.cloned.1.call-update) | async-done | bytes 49168 | tf_op jit(solution)/shard_map/reduce_scatter | solution.py:139
  228.8 1.5 convert_element_type.67
  230.2 39.5 %all-gather.6.cloned.1.call-done = bf16[96,8192]{1,0:T(8,128)(2,1)} async-done(((bf16[96,1024]{1,0:T(8,128)(2,1)}), bf16[96,8192]{1,0:T(8,128)(2,1)}) %all-gather.6.cloned.1.call-update) | async-done | bytes 1572880 | tf_op jit(solution)/shard_map/all_gather | solution.py:104
  269.8 2.8 fusion.17
  272.6 1.2 fusion.26
  274.1 1.2 fusion.38
  276.0 1.0 fusion.7
  (60 shorter events, 7.6 us)
Async XLA Ops:
  7.2 138.7 %copy-start = (bf16[96,128,128]{2,1,0:T(8,128)(2,1)S(1)}, bf16[96,128,128]{2,1,0:T(8,128)(2,1)}, u32[]{:S(2)}) copy-start(bf16[96,128,128]{2,1,0:T(8,128)(2,1)} %param.13) | copy-start | bytes 9437188
  7.2 59.3 %all-gather.8.cloned.1.call-start = ((), (), s32[]{:S(2)}) async-start(), calls=%async_computation.2 | async-start | bytes 6488064 | tf_op jit(solution)/shard_map/all_gather | solution.py:112
  7.9 124.2 %all-gather.10.cloned.1.call-start = ((), (), s32[]{:S(2)}) async-start(), calls=%async_computation.4 | async-start | bytes 1179648 | tf_op jit(solution)/shard_map/all_gather | solution.py:127
  84.3 9.4 %copy-start.1 = (bf16[4,2,64,128]{3,2,1,0:T(8,128)(2,1)S(1)}, bf16[4,2,64,128]{3,2,1,0:T(8,128)(2,1)}, u32[]{:S(2)}) copy-start(bf16[4,2,64,128]{3,2,1,0:T(8,128)(2,1)} %param.19) | copy-start | bytes 393220
  93.7 135.1 %reduce-scatter.2.cloned.1.call-start = ((), (), s32[]{:S(2)}) async-start(), calls=%async_computation.3 | async-start | bytes 1622016 | tf_op jit(solution)/shard_map/reduce_scatter | solution.py:139
  141.7 3.4 %copy-start.7 = (bf16[96,1024]{1,0:T(8,128)(2,1)S(1)}, bf16[96,1024]{1,0:T(8,128)(2,1)}, u32[]{:S(2)}) copy-start(bf16[96,1024]{1,0:T(8,128)(2,1)} %param.12) | copy-start | bytes 589828
  141.7 3.5 %copy-start.9 = (s32[96]{0:T(128)S(1)}, s32[96]{0:T(128)}, u32[]{:S(2)}) copy-start(s32[96]{0:T(128)} %param.15) | copy-start | bytes 1156
  144.5 125.3 %all-gather.6.cloned.1.call-start = ((), (), s32[]{:S(2)}) async-start(), calls=%async_computation.1 | async-start | bytes 1769472 | tf_op jit(solution)/shard_map/all_gather | solution.py:104
  145.1 0.7 copy-start.4
  269.8 4.0 %copy-start.5 = (f32[96,8]{1,0:T(8,128)S(1)}, f32[96,8]{1,0:T(8,128)}, u32[]{:S(2)}) copy-start(f32[96,8]{1,0:T(8,128)} %get-tuple-element.9) | copy-start | bytes 9220
  269.8 4.3 %copy-start.2 = (bf16[96,8192]{1,0:T(8,128)(2,1)S(1)}, bf16[96,8192]{1,0:T(8,128)(2,1)}, u32[]{:S(2)}) copy-start(bf16[96,8192]{1,0:T(8,128)(2,1)} %all-gather.6.cloned.1.call-done) | copy-start | bytes 4718596
  269.8 4.4 %copy-start.3 = (bf16[8192,128]{1,0:T(8,128)(2,1)S(1)}, bf16[8192,128]{1,0:T(8,128)(2,1)}, u32[]{:S(2)}) copy-start(bf16[8192,128]{1,0:T(8,128)(2,1)} %param.17) | copy-start | bytes 6291460
  269.8 4.4 %copy-start.6 = (f32[96,2,128]{2,0,1:T(8,128)S(1)}, f32[96,2,128]{2,0,1:T(8,128)}, u32[]{:S(2)}) copy-start(f32[96,2,128]{2,0,1:T(8,128)} %convert_element_type.67) | copy-start | bytes 294916
  272.5 2.8 copy-start.8
  274.1 1.9 copy-start.10
Sparse Core Ops, SparseCore 0:
  10.5 55.9 all-gather.7
  93.8 38.2 all-gather.9
  144.6 84.1 reduce-scatter.1
  230.4 39.2 all-gather.5
